TPU v7x, 256 devices: a whole 4x4x8 slice. The times are simulated.
256 devices in a mesh: tm: 32 (over y_hi, z, core), head: 8 (over y_lo, x).
Axes of the slice: x: 4, y: 4 (y_hi: 2, y_lo: 2; y = y_hi * 2 + y_lo), z: 8, core: 2. Of those that a mesh axis runs over, the one named last changes fastest.
Arguments:
- frames: bfloat16 [16384, 1024], P('tm'), may hold values from -8 to 8
- norm_gain: float32 [1024], replicated, may hold values from 0.5 to 1.5
- w_qkv: bfloat16 [3, 1024, 1024], P(None, 'tm', 'head'), may hold values from -6 to 6
- slopes: float32 [8], P('head'), may hold values from 1.5258789e-05 to 0.05
- w_out: bfloat16 [1024, 1024], P('head', 'tm'), may hold values from -0.5 to 0.5
Outputs:
- attended: bfloat16 [16384, 1024], P(('tm', 'head'))
All inputs are finite; a program needn't handle non-finite values.
Results may differ from a plain program's by a relative error of at most 0.014.
Values may be sent and summed in bfloat16 or wider, within the bound.
No kernel may reach another device: no remote copies, remote signals or barrier semaphores. Data moves between devices by JAX's collectives and lax.ppermute only.
A program may use at most 128 MiB of HBM per device.

v0:
```python
import jax
import jax.numpy as jnp
from jax import lax
from jax.sharding import PartitionSpec as P


def local(frames, norm_gain, w_qkv, slopes, w_out):
    frame_count = frames.shape[0]
    local_heads = slopes.shape[0]
    head_size = w_qkv.shape[2] // local_heads
    tm_count = lax.axis_size("tm")
    clip_len = frame_count * tm_count
    me_tm = lax.axis_index("tm")
    scale = head_size ** (-0.5)
    wide = frames.astype(jnp.float32)
    mean_square = jnp.mean(wide * wide, axis=-1, keepdims=True)
    inverse_root = lax.rsqrt(mean_square + 1e-06)
    normed = (wide * inverse_root * norm_gain).astype(jnp.bfloat16)
    projected = jnp.einsum(
        "rd,cde->cre",
        normed,
        lax.all_gather(w_qkv, "tm", axis=1, tiled=True),
        preferred_element_type=jnp.float32,
    ).astype(jnp.bfloat16)
    query = projected[0].reshape(frame_count, local_heads, head_size)
    keyed = projected[1].reshape(frame_count, local_heads, head_size)
    valued = projected[2].reshape(frame_count, local_heads, head_size)
    row_pos = me_tm * frame_count + jnp.arange(frame_count, dtype=jnp.int32)
    key_piece = lax.all_gather(keyed, "tm", axis=0, tiled=True)
    peak = jnp.full((local_heads, frame_count), -1e30, jnp.float32)
    scores = (
        jnp.einsum("qhd,khd->hqk", query, key_piece, preferred_element_type=jnp.float32) * scale
    )
    key_pos = jnp.arange(key_piece.shape[0], dtype=jnp.int32)
    differ = (key_pos[None, :] - row_pos[:, None]) % clip_len
    distance = jnp.minimum(differ, clip_len - differ).astype(jnp.float32)
    scores = scores - slopes[:, None, None] * distance[None, :, :]
    new_peak = jnp.maximum(peak, jnp.max(scores, axis=-1))
    expo = jnp.exp(scores - new_peak[:, :, None])
    totals = jnp.sum(expo, axis=-1)
    accum = jnp.einsum(
        "hqk,khd->hqd",
        expo.astype(jnp.bfloat16),
        lax.all_gather(valued, "tm", axis=0, tiled=True),
        preferred_element_type=jnp.float32,
    )
    state = (new_peak, totals, accum)
    peak, totals, accum = state
    mixed = (accum / totals[:, :, None]).astype(jnp.bfloat16)
    mixed = jnp.transpose(mixed, (1, 0, 2)).reshape(frame_count, local_heads * head_size)
    out_local = lax.all_gather(w_out, "tm", axis=1, tiled=True)
    return lax.psum_scatter(
        jnp.dot(mixed, out_local, preferred_element_type=jnp.float32).astype(jnp.bfloat16),
        "head",
        scatter_dimension=0,
        tiled=True,
    )


def solution(mesh):
    in_specs = (P("tm", None), P(), P(None, "tm", "head"), P("head"), P("head", "tm"))
    out_specs = P(("tm", "head"), None)
    return jax.shard_map(local, mesh=mesh, in_specs=in_specs, out_specs=out_specs, check_vma=False)
```

profile of v0, /device:TPU:32, one launch (start us, length us, event | category | flops | bytes accessed | tf_op | source)
XLA Modules:
  0.0 288.1 jit_solution(1928262164631459271)
XLA Ops:
  6.5 0.0 all-gather.5.cloned.1.call-start
  6.5 42.6 %all_gather.12 = bf16[3,1024,128]{2,1,0:T(8,128)(2,1)S(1)} all-gather(bf16[3,32,128]{2,1,0:T(8,128)(2,1)} %param.7), channel_id=1, replica_groups=mesh['tm'=32,'head'=8] {'tm'}, dimensions={1}, use_global_device_ids=true | all-gather | bytes 811008 | tf_op jit(solution)/shard_map/all_gather | solution.py:22
  49.2 1.5 fusion.14
  50.7 2.0 fusion.17
  52.7 0.7 fusion.37
  53.4 0.0 all-gather.5.cloned.1.call-update
  53.4 0.0 all-gather.7.cloned.1.call-start
  53.5 0.7 all-gather.7.cloned.1.call-update
  54.2 0.0 reduce-scatter.2.cloned.1.call-start
  54.9 42.0 %all_gather.15 = bf16[128,1024]{0,1:T(8,128)(2,1)S(1)} all-gather(bf16[128,32]{0,1:T(8,128)(2,1)} %param.9), channel_id=1, replica_groups=mesh['tm'=32,'head'=8] {'tm'}, dimensions={1}, use_global_device_ids=true | all-gather | bytes 270336 | tf_op jit(solution)/shard_map/all_gather | solution.py:51
  96.9 41.4 %all-gather.5.cloned.1.call-done = bf16[1,16384,128]{2,1,0:T(8,128)(2,1)} async-done(((bf16[1,512,128]{2,1,0:T(8,128)(2,1)}), bf16[1,16384,128]{2,1,0:T(8,128)(2,1)}) %all-gather.5.cloned.1.call-update) | async-done | bytes 4194320 | tf_op jit(solution)/shard_map/all_gather | solution.py:29
  138.2 29.7 %fusion.38 = (f32[512]{0:T(512)S(1)}, f32[512,16384]{1,0:T(8,128)}) fusion(s32[512]{0:T(512)S(1)} %iota_add_fusion, f32[]{:T(128)} %bitcast.27, bf16[1,16384,128]{2,1,0:T(8,128)(2,1)} %all-gather.5.cloned.1.call-done, bf16[3,512,128]{2,1,0:T(8,128)(2,1)S(1)} %fusion.17), kind=kOutput, calls=%fused_computation.37 | convolution fusion | flops 2306866688 | bytes 37883908 | tf_op jit(solution)/shard_map/qhd,khd->hqk/dot_general | solution.py:32
  168.0 13.8 %fusion.7 = f32[512]{0:T(512)S(1)} fusion(f32[512,16384]{1,0:T(8,128)} %get-tuple-element.8, f32[512]{0:T(512)S(1)} %broadcast_maximum_fusion), kind=kLoop, calls=%fused_computation.12 | loop fusion | flops 16776704 | bytes 33558528 | tf_op jit(solution)/shard_map/reduce_sum | solution.py:40
  181.8 42.5 %all-gather.7.cloned.1.call-done = bf16[1,16384,128]{2,1,0:T(8,128)(2,1)} async-done(((bf16[1,512,128]{2,1,0:T(8,128)(2,1)}), bf16[1,16384,128]{2,1,0:T(8,128)(2,1)}) %all-gather.7.cloned.1.call-update) | async-done | bytes 4194320 | tf_op jit(solution)/shard_map/all_gather | solution.py:44
  224.4 18.0 %convolution_convert_fusion = bf16[512,1024]{1,0:T(8,128)(2,1)} fusion(bf16[128,1024]{0,1:T(8,128)(2,1)S(1)} %all_gather.15, bf16[1,16384,128]{2,1,0:T(8,128)(2,1)} %all-gather.7.cloned.1.call-done, f32[512,16384]{1,0:T(8,128)} %get-tuple-element.8, f32[512]{0:T(512)S(1)} %broadcast_maximum_fusion, f32[512]{0:T(512)S(1)} %fusion.7), kind=kOutput, calls=%fused_computation.23 | convolution fusion | flops 2299133952 | bytes 39063552 | tf_op jit(solution)/shard_map/dot_general | solution.py:53
  242.4 0.0 reduce-scatter.2.cloned.1.call-update
  242.5 39.1 %reduce-scatter.2.cloned.1.call-done = bf16[64,1024]{1,0:T(8,128)(2,1)} async-done(((bf16[512,1024]{1,0:T(8,128)(2,1)}), bf16[64,1024]{1,0:T(8,128)(2,1)}) %reduce-scatter.2.cloned.1.call-update) | async-done | bytes 131088 | tf_op jit(solution)/shard_map/reduce_scatter | solution.py:52
  (3 shorter events, 0.0 us)
Async XLA Ops:
  6.5 131.7 %all-gather.5.cloned.1.call-start = ((), (), s32[]{:S(2)}) async-start(), calls=%async_computation.2 | async-start | bytes 4325376 | tf_op jit(solution)/shard_map/all_gather | solution.py:29
  53.4 171.0 %all-gather.7.cloned.1.call-start = ((), (), s32[]{:S(2)}) async-start(), calls=%async_computation.3 | async-start | bytes 4325376 | tf_op jit(solution)/shard_map/all_gather | solution.py:44
  54.2 227.4 %reduce-scatter.2.cloned.1.call-start = ((), (), s32[]{:S(2)}) async-start(), calls=%async_computation.1 | async-start | bytes 1179648 | tf_op jit(solution)/shard_map/reduce_scatter | solution.py:52
Sparse Core Ops, SparseCore 0:
  53.5 84.6 all-gather.4
  141.0 83.3 all-gather.6
  242.6 38.9 reduce-scatter.1
where the time goes:
time: 288 us
  waiting for transfers between devices  124 us (43%)
  blocking collectives  84.6 us (29%)
  matrix products  49.8 us (17%)
  other arithmetic  15.4 us (5%)
  between operations  13.8 us (5%)
    all_gather x1, blocking collectives, local(): lax.all_gather(w_qkv, 'tm', axis=1, tiled=True)  42.6 us
    all_gather x1, waiting for transfers between devices, local(): lax.all_gather(valued, 'tm', axis=0, tiled=True)  42.5 us
    all_gather x1, blocking collectives, local(): out_local = lax.all_gather(w_out, 'tm', axis=1, tiled=True)  42 us
    all_gather x1, waiting for transfers between devices, local(): key_piece = lax.all_gather(keyed, 'tm', axis=0, tiled=True)  41.4 us
    reduce_scatter x1, waiting for transfers between devices, local(): lax.psum_scatter(jnp.dot(mixed, out_local, preferred_element_type=jnp.flo...  39.1 us
    dot_general x1, matrix products, local(): jnp.einsum('qhd,khd->hqk', query, key_piece, preferred_element_type=jnp.f...  29.7 us
    dot_general x1, matrix products, local(): jnp.dot(mixed, out_local, preferred_element_type=jnp.float32)  18 us
    reduce_sum x1, other arithmetic, local(): totals = jnp.sum(expo, axis=-1)  13.8 us
  transfers between devices with their start and end apart: 3, of which 3 were waited for; matrix products, arithmetic and copies ran while one was open for 15% of the time, Pallas kernels for 0%

commit v1 on v0

--- a/solution.py
+++ b/solution.py
@@ -2,6 +2,14 @@
 import jax.numpy as jnp
 from jax import lax
 from jax.sharding import PartitionSpec as P
+
+
+def run_the_plate(mine):
+    outer = lax.axis_size("tm")
+    side_arr = jnp.stack(outer * [mine])
+    low = lax.all_to_all(side_arr, axis_name="tm", split_axis=0, concat_axis=0)
+    back = jnp.concatenate(low, 1)
+    return back
 
 
 def local(frames, norm_gain, w_qkv, slopes, w_out):
@@ -17,10 +25,7 @@
     inverse_root = lax.rsqrt(mean_square + 1e-06)
     normed = (wide * inverse_root * norm_gain).astype(jnp.bfloat16)
     projected = jnp.einsum(
-        "rd,cde->cre",
-        normed,
-        lax.all_gather(w_qkv, "tm", axis=1, tiled=True),
-        preferred_element_type=jnp.float32,
+        "rd,cde->cre", normed, run_the_plate(w_qkv), preferred_element_type=jnp.float32
     ).astype(jnp.bfloat16)
     query = projected[0].reshape(frame_count, local_heads, head_size)
     keyed = projected[1].reshape(frame_count, local_heads, head_size)

time: 288 us -> 279 us (0.969)
  blocking collectives: 84.6 us -> 37.7 us
  waiting for transfers between devices: 124 us -> 148 us
  starting transfers between devices: 0.08 us -> 11.5 us
    all_gather x1 -> x0, blocking collectives: 42.6 us -> none  [local(): lax.all_gather(w_qkv, 'tm', axis=1, tiled=True)]
    all_to_all x0 -> x1, waiting for transfers between devices: none -> 23.3 us  [run_the_plate(): low = lax.all_to_all(side_arr, axis_name='tm', split_axis=0, concat_axis=0)]
    all_to_all x0 -> x1, starting transfers between devices: none -> 11.4 us  [run_the_plate(): low = lax.all_to_all(side_arr, axis_name='tm', split_axis=0, concat_axis=0)]
    all_gather x1, blocking collectives: 42 us -> 37.7 us  [local(): out_local = lax.all_gather(w_out, 'tm', axis=1, tiled=True)]
  transfers between devices with their start and end apart: 3 -> 4, of which waited for: 3 -> 4; matrix products, arithmetic and copies ran while one was open for 15% -> 16% of each run, Pallas kernels for 0% -> 0%
where the time goes in v1:
time: 279 us; the launch traced here: 278 us
  waiting for transfers between devices  148 us (53%)
  matrix products  49.8 us (18%)
  blocking collectives  37.7 us (14%)
  other arithmetic  15.4 us (6%)
  between operations  13.8 us (5%)
  starting transfers between devices  11.5 us (4%)
    all_gather x1, waiting for transfers between devices, local(): lax.all_gather(valued, 'tm', axis=0, tiled=True)  42.5 us
    all_gather x1, waiting for transfers between devices, local(): key_piece = lax.all_gather(keyed, 'tm', axis=0, tiled=True)  42.3 us
    reduce_scatter x1, waiting for transfers between devices, local(): lax.psum_scatter(jnp.dot(mixed, out_local, preferred_element_type=jnp.flo...  39.1 us
    all_gather x1, blocking collectives, local(): out_local = lax.all_gather(w_out, 'tm', axis=1, tiled=True)  37.7 us
    dot_general x1, matrix products, local(): jnp.einsum('qhd,khd->hqk', query, key_piece, preferred_element_type=jnp.f...  29.7 us
    all_to_all x1, waiting for transfers between devices, run_the_plate(): low = lax.all_to_all(side_arr, axis_name='tm', split_axis=0, concat_axis=0)  23.3 us
    dot_general x1, matrix products, local(): jnp.dot(mixed, out_local, preferred_element_type=jnp.float32)  18 us
    reduce_sum x1, other arithmetic, local(): totals = jnp.sum(expo, axis=-1)  13.8 us
  transfers between devices with their start and end apart: 4, of which 4 were waited for; matrix products, arithmetic and copies ran while one was open for 16% of the time, Pallas kernels for 0%

profile of v1, /device:TPU:32, one launch (start us, length us, event | category | flops | bytes accessed | tf_op | source)
XLA Modules:
  0.0 278.5 jit_solution(472481001580351591)
XLA Ops:
  6.5 1.7 stack.2
  8.3 11.4 %all-to-all-start = ((bf16[32,3,32,128]{3,2,1,0:T(8,128)(2,1)}), bf16[32,3,32,128]{3,2,1,0:T(8,128)(2,1)S(1)}, u32[]{:S(2)}, u32[]{:S(2)}) async-start(bf16[32,3,32,128]{3,2,1,0:T(8,128)(2,1)} %stack.2), calls=%async_computation | async-start | bytes 1572864 | tf_op jit(solution)/shard_map/all_to_all | solution.py:10
  19.6 0.0 all-gather.5.cloned.1.call-start
  19.7 1.5 fusion.14
  21.2 23.3 %all-to-all-done = bf16[32,3,32,128]{3,2,1,0:T(8,128)(2,1)S(1)} async-done(((bf16[32,3,32,128]{3,2,1,0:T(8,128)(2,1)}), bf16[32,3,32,128]{3,2,1,0:T(8,128)(2,1)S(1)}, u32[]{:S(2)}, u32[]{:S(2)}) %all-to-all-start) | async-done | bytes 786464 | tf_op jit(solution)/shard_map/all_to_all | solution.py:10
  44.5 0.1 copy.6
  44.5 2.0 fusion.17
  46.5 0.7 fusion.37
  47.2 0.0 all-gather.5.cloned.1.call-update
  47.2 0.0 all-gather.7.cloned.1.call-start
  47.3 0.7 all-gather.7.cloned.1.call-update
  48.0 0.0 reduce-scatter.2.cloned.1.call-start
  48.7 37.7 %all_gather.11 = bf16[128,1024]{0,1:T(8,128)(2,1)S(1)} all-gather(bf16[128,32]{0,1:T(8,128)(2,1)} %param.9), channel_id=1, replica_groups=mesh['tm'=32,'head'=8] {'tm'}, dimensions={1}, use_global_device_ids=true | all-gather | bytes 270336 | tf_op jit(solution)/shard_map/all_gather | solution.py:56
  86.4 42.3 %all-gather.5.cloned.1.call-done = bf16[1,16384,128]{2,1,0:T(8,128)(2,1)} async-done(((bf16[1,512,128]{2,1,0:T(8,128)(2,1)}), bf16[1,16384,128]{2,1,0:T(8,128)(2,1)}) %all-gather.5.cloned.1.call-update) | async-done | bytes 4194320 | tf_op jit(solution)/shard_map/all_gather | solution.py:34
  128.7 29.7 %fusion.38 = (f32[512]{0:T(512)S(1)}, f32[512,16384]{1,0:T(8,128)}) fusion(s32[512]{0:T(512)S(1)} %iota_add_fusion, f32[]{:T(128)} %bitcast.29, bf16[1,16384,128]{2,1,0:T(8,128)(2,1)} %all-gather.5.cloned.1.call-done, bf16[3,512,128]{2,1,0:T(8,128)(2,1)S(1)} %fusion.17), kind=kOutput, calls=%fused_computation.37 | convolution fusion | flops 2306866688 | bytes 37883908 | tf_op jit(solution)/shard_map/qhd,khd->hqk/dot_general | solution.py:37
  158.4 13.8 %fusion.7 = f32[512]{0:T(512)S(1)} fusion(f32[512,16384]{1,0:T(8,128)} %get-tuple-element.8, f32[512]{0:T(512)S(1)} %broadcast_maximum_fusion), kind=kLoop, calls=%fused_computation.12 | loop fusion | flops 16776704 | bytes 33558528 | tf_op jit(solution)/shard_map/reduce_sum | solution.py:45
  172.3 42.5 %all-gather.7.cloned.1.call-done = bf16[1,16384,128]{2,1,0:T(8,128)(2,1)} async-done(((bf16[1,512,128]{2,1,0:T(8,128)(2,1)}), bf16[1,16384,128]{2,1,0:T(8,128)(2,1)}) %all-gather.7.cloned.1.call-update) | async-done | bytes 4194320 | tf_op jit(solution)/shard_map/all_gather | solution.py:49
  214.7 18.0 %convolution_convert_fusion = bf16[512,1024]{1,0:T(8,128)(2,1)} fusion(bf16[128,1024]{0,1:T(8,128)(2,1)S(1)} %all_gather.11, bf16[1,16384,128]{2,1,0:T(8,128)(2,1)} %all-gather.7.cloned.1.call-done, f32[512,16384]{1,0:T(8,128)} %get-tuple-element.8, f32[512]{0:T(512)S(1)} %broadcast_maximum_fusion, f32[512]{0:T(512)S(1)} %fusion.7), kind=kOutput, calls=%fused_computation.23 | convolution fusion | flops 2299133952 | bytes 39063552 | tf_op jit(solution)/shard_map/dot_general | solution.py:58
  232.8 0.0 reduce-scatter.2.cloned.1.call-update
  232.8 39.1 %reduce-scatter.2.cloned.1.call-done = bf16[64,1024]{1,0:T(8,128)(2,1)} async-done(((bf16[512,1024]{1,0:T(8,128)(2,1)}), bf16[64,1024]{1,0:T(8,128)(2,1)}) %reduce-scatter.2.cloned.1.call-update) | async-done | bytes 131088 | tf_op jit(solution)/shard_map/reduce_scatter | solution.py:57
  (3 shorter events, 0.0 us)
Async XLA Ops:
  8.3 36.2 %all-to-all-start = ((bf16[32,3,32,128]{3,2,1,0:T(8,128)(2,1)}), bf16[32,3,32,128]{3,2,1,0:T(8,128)(2,1)S(1)}, u32[]{:S(2)}, u32[]{:S(2)}) async-start(bf16[32,3,32,128]{3,2,1,0:T(8,128)(2,1)} %stack.2), calls=%async_computation | async-start | bytes 1572864 | tf_op jit(solution)/shard_map/all_to_all | solution.py:10
  19.6 109.0 %all-gather.5.cloned.1.call-start = ((), (), s32[]{:S(2)}) async-start(), calls=%async_computation.3 | async-start | bytes 4325376 | tf_op jit(solution)/shard_map/all_gather | solution.py:34
  47.2 167.5 %all-gather.7.cloned.1.call-start = ((), (), s32[]{:S(2)}) async-start(), calls=%async_computation.4 | async-start | bytes 4325376 | tf_op jit(solution)/shard_map/all_gather | solution.py:49
  48.0 224.0 %reduce-scatter.2.cloned.1.call-start = ((), (), s32[]{:S(2)}) async-start(), calls=%async_computation.2 | async-start | bytes 1179648 | tf_op jit(solution)/shard_map/reduce_scatter | solution.py:57
Sparse Core Ops, SparseCore 0:
  47.4 81.2 all-gather.4
  131.4 83.2 all-gather.6
  232.9 38.9 reduce-scatter.1
